TPU v7x, 128 devices: a whole 4x4x4 slice. The times are simulated.
128 devices in a mesh: dp: 32 (over z_lo, y, x), mp: 4 (over z_hi, core).
Axes of the slice: x: 4, y: 4, z: 4 (z_hi: 2, z_lo: 2; z = z_hi * 2 + z_lo), core: 2. Of those that a mesh axis runs over, the one named last changes fastest.
Arguments:
- queries: bfloat16 [20480, 4096], P('dp', 'mp'), may hold values from -180 to 180
- keys: bfloat16 [20480, 512], P('dp', 'mp'), may hold values from -6 to 6
- values: bfloat16 [20480, 512], P('dp', 'mp'), may hold values from -6 to 6
- prompt_keys: bfloat16 [128, 512], P(None, 'mp'), may hold values from -6 to 6
- prompt_values: bfloat16 [128, 512], P(None, 'mp'), may hold values from -6 to 6
- out_weight: bfloat16 [4096, 8192], P('mp', 'dp'), may hold values from -0.09375 to 0.09375
- out_grad: bfloat16 [20480, 8192], P('dp'), may hold values from -6 to 6
- lengths: int32 [32, 8], P('dp'), may hold values from 1 to 320, 640 in all within a row
Outputs:
- mixed: bfloat16 [20480, 8192], P('dp', 'mp')
- prompt_key_grad: float32 [128, 512], P('dp', 'mp')
- prompt_value_grad: float32 [128, 512], P('dp', 'mp')
All inputs are finite; a program needn't handle non-finite values.
Results may differ from a plain program's by a relative error of at most 0.024.
Values may be sent and summed in bfloat16 or wider, within the bound.
A program may use at most 192 MiB of HBM per device.

v0:
```python
import jax
import jax.numpy as jnp
from jax import lax
from jax.sharding import PartitionSpec as P

HD = 128
rope_base = 1000000.0


def split_up(x, dim, length):
    dims = x.shape
    parts = x.reshape(*dims[:dim], length, dims[dim] // length, *dims[dim + 1 :])
    return jnp.moveaxis(parts, dim, 0)


def sum_at_owner(x, axis, dim):
    length = lax.axis_size(axis)
    parts = lax.all_to_all(split_up(x, dim, length), axis, 0, 0, tiled=True)
    return jnp.sum(parts.astype(jnp.float32), axis=0)


def sent_together(arrays, axis, dim, along):
    both = jnp.concatenate(arrays, axis=along)
    filled, at, finished = (sum_at_owner(both, axis, dim), 0, [])
    for a in arrays:
        finished.append(lax.slice_in_dim(filled, at, at + a.shape[along], axis=along))
        at += a.shape[along]
    return tuple(finished)


def doc_layout(lens, count):
    ends = jnp.cumsum(lens)
    starts = ends - lens
    index = jnp.arange(count, dtype=jnp.int32)
    segment = jnp.sum((index[:, None] >= ends[None, :]).astype(jnp.int32), axis=1)
    doc_ids = jnp.arange(lens.shape[0], dtype=jnp.int32)
    offset = jnp.sum(jnp.where(segment[:, None] == doc_ids[None, :], starts[None, :], 0), axis=1)
    return (segment, index - offset)


def rotate(field, position):
    half = HD // 2
    freq = rope_base ** (-2.0 * jnp.arange(half, dtype=jnp.float32) / HD)
    angle = position.astype(jnp.float32)[:, None] * freq[None, :]
    cosine = jnp.cos(angle)[:, None, :]
    sine = jnp.sin(angle)[:, None, :]
    first = field[..., :half].astype(jnp.float32)
    second = field[..., half:].astype(jnp.float32)
    return jnp.concatenate(
        [first * cosine - second * sine, second * cosine + first * sine], axis=-1
    ).astype(jnp.bfloat16)


def per_device(queries, keys, values, prompt_keys, prompt_values, out_weight, out_grad, lengths):
    tok_rows = queries.shape[0]
    kv_local = keys.shape[1] // HD
    groups = queries.shape[1] // HD // kv_local
    prompt_rows = prompt_keys.shape[0]
    scale = HD ** (-0.5)
    segment, position = doc_layout(lengths[0], tok_rows)
    q_rot = rotate(queries.reshape(tok_rows, kv_local * groups, HD), position).reshape(
        tok_rows, kv_local, groups, HD
    )
    k_rot = rotate(keys.reshape(tok_rows, kv_local, HD), position)
    key_all = jnp.concatenate([prompt_keys.reshape(prompt_rows, kv_local, HD), k_rot], axis=0)
    value_all = jnp.concatenate(
        [prompt_values.reshape(prompt_rows, kv_local, HD), values.reshape(tok_rows, kv_local, HD)],
        axis=0,
    )
    index = jnp.arange(tok_rows, dtype=jnp.int32)
    own = (segment[:, None] == segment[None, :]) & (index[None, :] <= index[:, None])
    key_mask = jnp.concatenate([jnp.ones((tok_rows, prompt_rows), dtype=bool), own], axis=1)
    scores = (
        jnp.einsum("tkgd,skd->kgts", q_rot, key_all, preferred_element_type=jnp.float32) * scale
    )
    scores = jnp.where(key_mask[None, None], scores, -1e30)
    shifted = jnp.exp(scores - jnp.max(scores, axis=-1, keepdims=True))
    shifted = jnp.where(key_mask[None, None], shifted, 0.0)
    probs = shifted / jnp.sum(shifted, axis=-1, keepdims=True)
    probs_b = probs.astype(jnp.bfloat16)
    attn = jnp.einsum("kgts,skd->tkgd", probs_b, value_all, preferred_element_type=jnp.float32)
    attn = attn.astype(jnp.bfloat16).reshape(tok_rows, kv_local * groups * HD)
    partial_value = jnp.dot(
        attn,
        lax.all_gather(out_weight, "dp", axis=1, tiled=True),
        preferred_element_type=jnp.float32,
    )
    grad_total = lax.dot_general(
        out_grad,
        lax.all_gather(out_weight, "dp", axis=1, tiled=True),
        (((1,), (1,)), ((), ())),
        preferred_element_type=jnp.float32,
    )
    mixed = lax.psum_scatter(
        partial_value.astype(jnp.bfloat16), "mp", scatter_dimension=1, tiled=True
    )
    grad_attn = grad_total.astype(jnp.bfloat16).reshape(tok_rows, kv_local, groups, HD)
    value_grad = jnp.einsum(
        "kgts,tkgd->skd", probs_b[..., :prompt_rows], grad_attn, preferred_element_type=jnp.float32
    )
    grad_probs = jnp.einsum(
        "tkgd,skd->kgts", grad_attn, value_all, preferred_element_type=jnp.float32
    )
    d_scores = probs * (grad_probs - jnp.sum(probs * grad_probs, axis=-1, keepdims=True)) * scale
    d_scores = d_scores.astype(jnp.bfloat16)
    key_grad = jnp.einsum(
        "kgts,tkgd->skd", d_scores[..., :prompt_rows], q_rot, preferred_element_type=jnp.float32
    )
    owned = sent_together(
        (
            key_grad.reshape(prompt_rows, kv_local * HD).astype(jnp.bfloat16),
            value_grad.reshape(prompt_rows, kv_local * HD).astype(jnp.bfloat16),
        ),
        "dp",
        0,
        1,
    )
    return (mixed, owned[0], owned[1])


def solution(mesh):
    in_specs = (
        P("dp", "mp"),
        P("dp", "mp"),
        P("dp", "mp"),
        P(None, "mp"),
        P(None, "mp"),
        P("mp", "dp"),
        P("dp", None),
        P("dp", None),
    )
    out_specs = (P("dp", "mp"), P("dp", "mp"), P("dp", "mp"))
    return jax.shard_map(
        per_device, mesh=mesh, in_specs=in_specs, out_specs=out_specs, check_vma=False
    )
```

profile of v0, /device:TPU:1, one launch (start us, length us, event | category | flops | bytes accessed | tf_op | source)
XLA Modules:
  0.0 424.6 jit_solution(10789679038603178659)
XLA Ops:
  7.2 0.7 all-gather.2.cloned.1.call-update
  7.9 1.7 copy.39
  9.8 1.4 copy.52
  11.3 1.4 copy.53
  13.6 0.3 fusion.11
  14.0 0.7 fusion.37
  14.8 1.2 multiply_cosine_fusion
  16.0 2.2 fusion.6
  18.1 7.5 %fusion = (f32[8,640]{1,0:T(8,128)S(1)}, f32[768,640,8]{1,0,2:T(8,128)}) fusion(pred[640,768]{0,1:T(8,128)(4,1)S(1)} %concatenate.33, bf16[640,8,64]{2,0,1:T(8,128)(2,1)S(1)} %get-tuple-element.6, bf16[640,8,64]{2,0,1:T(8,128)(2,1)S(1)} %get-tuple-element.5, bf16[640,1,64]{0,2,1:T(8,128)(2,1)S(1)} %get-tuple-element.10, ...), kind=kOutput, calls=%fused_computation.3 | convolution fusion | flops 1021635584 | bytes 17747968 | tf_op jit(solution)/shard_map/tkgd,skd->kgts/dot_general | solution.py:74
  25.7 9.3 %fusion.2 = f32[8,640]{1,0:T(8,128)S(1)} fusion(f32[768,640,8]{1,0,2:T(8,128)} %get-tuple-element.16, f32[8,640]{1,0:T(8,128)S(1)} %get-tuple-element.15, pred[640,768]{0,1:T(8,128)(4,1)S(1)} %concatenate.33), kind=kLoop, calls=%fused_computation.6 | loop fusion | flops 19655680 | bytes 16261120 | tf_op jit(solution)/shard_map/reduce_sum | solution.py:79
  35.0 203.2 %all-gather.2.cloned.1.call-done = bf16[1024,8192]{1,0:T(8,128)(2,1)} async-done(((bf16[1024,256]{1,0:T(8,128)(2,1)}), bf16[1024,8192]{1,0:T(8,128)(2,1)}) %all-gather.2.cloned.1.call-update) | async-done | bytes 16777232 | tf_op jit(solution)/shard_map/all_gather | solution.py:85
  238.2 17.4 %convolution_convert_fusion.1 = bf16[640,1024]{1,0:T(8,128)(2,1)} fusion(bf16[640,8192]{1,0:T(8,128)(2,1)} %param.14, bf16[1024,8192]{1,0:T(8,128)(2,1)} %all-gather.2.cloned.1.call-done), kind=kOutput, calls=%fused_computation.25 | convolution fusion | flops 10738073600 | bytes 28573696 | tf_op jit(solution)/shard_map/dot_general | solution.py:88
  255.6 17.4 %multiply_reduce_fusion = (f32[8,640]{1,0:T(8,128)S(1)}, f32[1,8,640,768]{2,3,1,0:T(8,128)}, f32[1,8,640,768]{2,3,1,0:T(8,128)}) fusion(f32[8,640]{1,0:T(8,128)S(1)} %fusion.2, f32[8,640]{1,0:T(8,128)S(1)} %get-tuple-element.15, f32[768,640,8]{1,0,2:T(8,128)} %get-tuple-element.16, pred[640,768]{0,1:T(8,128)(4,1)S(1)} %concatenate.33, ...), kind=kOutput, calls=%fused_computation.1 | convolution fusion | flops 1034546176 | bytes 49246208 | tf_op jit(solution)/shard_map/tkgd,skd->kgts/dot_general | solution.py:101
  273.0 9.4 %convert_element_type.92 = bf16[1,8,640,768]{2,3,1,0:T(8,128)(2,1)} convert(f32[1,8,640,768]{2,3,1,0:T(8,128)} %get-tuple-element.4) | non-fusion elementwise | flops 3932160 | bytes 23592960 | tf_op jit(solution)/shard_map/convert_element_type | solution.py:80
  282.4 4.4 %fusion.12 = bf16[128,8,640]{2,0,1:T(8,128)(2,1)S(1)} fusion(bf16[1,8,640,768]{2,3,1,0:T(8,128)(2,1)} %convert_element_type.92, bf16[640,1,128]{0,2,1:T(8,128)(2,1)S(1)} %bitcast.106, bf16[128,1,128]{0,2,1:T(8,128)(2,1)S(1)} %bitcast.108), kind=kOutput, calls=%fused_computation.24 | convolution fusion | flops 1007681536 | bytes 9371648 | tf_op jit(solution)/shard_map/kgts,skd->tkgd/dot_general | solution.py:81
  286.8 19.5 %convolution_convert_fusion = bf16[640,8192]{1,0:T(8,128)(2,1)} fusion(bf16[640,1024]{0,1:T(8,128)(2,1)S(1)} %bitcast.102, bf16[1024,8192]{1,0:T(8,128)(2,1)} %all-gather.2.cloned.1.call-done), kind=kOutput, calls=%fused_computation.4 | convolution fusion | flops 10742661120 | bytes 28573696 | tf_op jit(solution)/shard_map/dot_general | solution.py:83
  306.4 2.5 slice_bitcast_fusion
  308.9 2.8 copy.46
  311.7 1.8 copy.55
  313.5 0.6 fusion.23
  314.1 3.7 fusion.24
  317.8 14.4 %all_to_all.5 = bf16[32,4,256]{2,1,0:T(4,128)(2,1)S(1)} all-to-all(bf16[32,4,256]{2,1,0:T(4,128)(2,1)S(1)} %pad_maximum_fusion.3), channel_id=1, replica_groups=mesh['dp'=32,'mp'=4] {'dp'}, dimensions={0} | all-to-all | bytes 131072 | tf_op jit(solution)/shard_map/all_to_all | solution.py:18
  332.3 0.6 fusion.48
  332.9 84.9 %reduce-scatter.2.cloned.1.call-done = bf16[640,2048]{1,0:T(8,128)(2,1)} async-done(((bf16[640,8192]{1,0:T(8,128)(2,1)}), bf16[640,2048]{1,0:T(8,128)(2,1)}) %reduce-scatter.2.cloned.1.call-update) | async-done | bytes 2621456 | tf_op jit(solution)/shard_map/reduce_scatter | solution.py:94
  (31 shorter events, 1.3 us)
Async XLA Ops:
  7.2 231.0 %all-gather.2.cloned.1.call-start = ((), (), s32[]{:S(2)}) async-start(), calls=%async_computation.2 | async-start | bytes 17301504 | tf_op jit(solution)/shard_map/all_gather | solution.py:85
  7.9 409.9 %reduce-scatter.2.cloned.1.call-start = ((), (), s32[]{:S(2)}) async-start(), calls=%async_computation.3 | async-start | bytes 13107200 | tf_op jit(solution)/shard_map/reduce_scatter | solution.py:94
  9.8 2.9 copy-start.2
  9.8 3.1 copy-start.4
  9.8 3.2 copy-start.3
  9.8 3.3 copy-start.5
  9.8 3.4 copy-start.6
  13.5 2.5 copy-start.1
  311.7 1.8 copy-start
Sparse Core Ops, SparseCore 0:
  9.6 228.5 all-gather.1
  306.5 111.1 reduce-scatter.1
where the time goes:
time: 425 us
  waiting for transfers between devices  289 us (68%)
  matrix products  70.5 us (17%)
  other arithmetic  23.5 us (6%)
  blocking collectives  14.4 us (3%)
  between operations  14.3 us (3%)
  local copies, waits for them, and re-layouts  13 us (3%)
    all_gather x1, waiting for transfers between devices, per_device(): lax.all_gather(out_weight, 'dp', axis=1, tiled=True)  203 us
    reduce_scatter x1, waiting for transfers between devices, per_device(): lax.psum_scatter(partial_value.astype(jnp.bfloat16), 'mp', scatter_dimens...  84.9 us
    dot_general x1, matrix products, per_device(): jnp.dot(attn, lax.all_gather(out_weight, 'dp', axis=1, tiled=True), prefe...  19.5 us
    dot_general x1, matrix products, per_device(): lax.dot_general(out_grad, lax.all_gather(out_weight, 'dp', axis=1, tiled=...  17.4 us
    dot_general x1, matrix products, per_device(): jnp.einsum('tkgd,skd->kgts', grad_attn, value_all, preferred_element_type...  17.4 us
    all_to_all x1, blocking collectives, sum_at_owner(): parts = lax.all_to_all(split_up(x, dim, length), axis, 0, 0, tiled=True)  14.4 us
    convert_element_type x1, other arithmetic, per_device(): probs_b = probs.astype(jnp.bfloat16)  9.41 us
    reduce_sum x1, other arithmetic, per_device(): probs = shifted / jnp.sum(shifted, axis=-1, keepdims=True)  9.28 us
  transfers between devices with their start and end apart: 2, of which 2 were waited for; matrix products, arithmetic and copies ran while one was open for 9% of the time, Pallas kernels for 0%

commit v1 on v0

--- a/solution.py
+++ b/solution.py
@@ -5,6 +5,11 @@
 
 HD = 128
 rope_base = 1000000.0
+
+
+def all_by_exchange(value, axis, d):
+    stack = jnp.stack([value] * lax.axis_size(axis))
+    return jnp.concatenate(lax.all_to_all(stack, axis, 0, 0), axis=d)
 
 
 def split_up(x, dim, length):
@@ -81,9 +86,7 @@
     attn = jnp.einsum("kgts,skd->tkgd", probs_b, value_all, preferred_element_type=jnp.float32)
     attn = attn.astype(jnp.bfloat16).reshape(tok_rows, kv_local * groups * HD)
     partial_value = jnp.dot(
-        attn,
-        lax.all_gather(out_weight, "dp", axis=1, tiled=True),
-        preferred_element_type=jnp.float32,
+        attn, all_by_exchange(out_weight, "dp", 1), preferred_element_type=jnp.float32
     )
     grad_total = lax.dot_general(
         out_grad,

time: 425 us -> 634 us (1.49)
  waiting for transfers between devices: 289 us -> 481 us
  starting transfers between devices: 0.08 us -> 9.56 us
  local copies, waits for them, and re-layouts: 13 us -> 19.4 us
    all_gather x1, waiting for transfers between devices: 203 us -> 400 us  [per_device(): lax.all_gather(out_weight, 'dp', axis=1, tiled=True)]
    all_to_all x0 -> x1, starting transfers between devices: none -> 9.48 us  [all_by_exchange(): return jnp.concatenate(lax.all_to_all(stack, axis, 0, 0), axis=d)]
  transfers between devices with their start and end apart: 2 -> 3, of which waited for: 2 -> 2; matrix products, arithmetic and copies ran while one was open for 9% -> 15% of each run, Pallas kernels for 0% -> 0%
where the time goes in v1:
time: 634 us; the launch traced here: 633 us
  waiting for transfers between devices  481 us (76%)
  matrix products  69.4 us (11%)
  other arithmetic  23.5 us (4%)
  local copies, waits for them, and re-layouts  19.4 us (3%)
  blocking collectives  16 us (3%)
  between operations  14.3 us (2%)
  starting transfers between devices  9.56 us (2%)
    all_gather x1, waiting for transfers between devices, per_device(): lax.all_gather(out_weight, 'dp', axis=1, tiled=True)  400 us
    reduce_scatter x1, waiting for transfers between devices, per_device(): lax.psum_scatter(partial_value.astype(jnp.bfloat16), 'mp', scatter_dimens...  80.6 us
    dot_general x1, matrix products, per_device(): lax.dot_general(out_grad, lax.all_gather(out_weight, 'dp', axis=1, tiled=...  17.4 us
    dot_general x1, matrix products, per_device(): jnp.dot(attn, all_by_exchange(out_weight, 'dp', 1), preferred_element_typ...  17.3 us
    dot_general x1, matrix products, per_device(): jnp.einsum('tkgd,skd->kgts', grad_attn, value_all, preferred_element_type...  17.3 us
    all_to_all x1, blocking collectives, sum_at_owner(): parts = lax.all_to_all(split_up(x, dim, length), axis, 0, 0, tiled=True)  16 us
  transfers between devices with their start and end apart: 3, of which 2 were waited for; matrix products, arithmetic and copies ran while one was open for 15% of the time, Pallas kernels for 0%

profile of v1, /device:TPU:1, one launch (start us, length us, event | category | flops | bytes accessed | tf_op | source)
XLA Modules:
  0.0 633.3 jit_solution(18145994821524665523)
XLA Ops:
  7.2 0.7 all-gather.2.cloned.1.call-update
  7.9 1.2 copy.46
  9.2 6.0 stack.2
  15.1 9.5 %all-to-all-start = ((bf16[32,1024,256]{1,2,0:T(8,128)(2,1)}), bf16[32,1024,256]{1,2,0:T(8,128)(2,1)}, u32[]{:S(2)}, u32[]{:S(2)}) async-start(bf16[32,1024,256]{1,2,0:T(8,128)(2,1)} %stack.2), calls=%async_computation | async-start | bytes 33554432 | tf_op jit(solution)/shard_map/all_to_all | solution.py:12
  24.7 0.7 copy.41
  25.6 1.4 copy.55
  27.0 1.4 copy.56
  29.8 0.7 fusion.37
  30.5 1.2 multiply_cosine_fusion
  31.8 2.2 fusion.6
  33.9 7.6 %fusion = (f32[8,640]{1,0:T(8,128)S(1)}, f32[768,640,8]{1,0,2:T(8,128)}) fusion(pred[640,768]{0,1:T(8,128)(4,1)S(1)} %concatenate.33, bf16[640,8,64]{2,0,1:T(8,128)(2,1)S(1)} %get-tuple-element.6, bf16[640,8,64]{2,0,1:T(8,128)(2,1)S(1)} %get-tuple-element.5, bf16[640,1,64]{0,2,1:T(8,128)(2,1)S(1)} %get-tuple-element.10, ...), kind=kOutput, calls=%fused_computation.3 | convolution fusion | flops 1021635584 | bytes 17747968 | tf_op jit(solution)/shard_map/tkgd,skd->kgts/dot_general | solution.py:79
  41.6 9.3 %fusion.2 = f32[8,640]{1,0:T(8,128)S(1)} fusion(f32[768,640,8]{1,0,2:T(8,128)} %get-tuple-element.16, f32[8,640]{1,0:T(8,128)S(1)} %get-tuple-element.15, pred[640,768]{0,1:T(8,128)(4,1)S(1)} %concatenate.33), kind=kLoop, calls=%fused_computation.6 | loop fusion | flops 19655680 | bytes 16261120 | tf_op jit(solution)/shard_map/reduce_sum | solution.py:84
  50.8 399.8 %all-gather.2.cloned.1.call-done = bf16[1024,8192]{1,0:T(8,128)(2,1)} async-done(((bf16[1024,256]{1,0:T(8,128)(2,1)}), bf16[1024,8192]{1,0:T(8,128)(2,1)}) %all-gather.2.cloned.1.call-update) | async-done | bytes 16777232 | tf_op jit(solution)/shard_map/all_gather | solution.py:93
  450.7 17.4 %convolution_convert_fusion.1 = bf16[640,1024]{1,0:T(8,128)(2,1)} fusion(bf16[640,8192]{1,0:T(8,128)(2,1)} %param.14, bf16[1024,8192]{1,0:T(8,128)(2,1)} %all-gather.2.cloned.1.call-done), kind=kOutput, calls=%fused_computation.25 | convolution fusion | flops 10738073600 | bytes 28573696 | tf_op jit(solution)/shard_map/dot_general | solution.py:91
  468.1 17.3 %multiply_reduce_fusion = (f32[8,640]{1,0:T(8,128)S(1)}, f32[1,8,640,768]{2,3,1,0:T(8,128)}, f32[1,8,640,768]{2,3,1,0:T(8,128)}) fusion(f32[8,640]{1,0:T(8,128)S(1)} %fusion.2, f32[8,640]{1,0:T(8,128)S(1)} %get-tuple-element.15, f32[768,640,8]{1,0,2:T(8,128)} %get-tuple-element.16, pred[640,768]{0,1:T(8,128)(4,1)S(1)} %concatenate.33, ...), kind=kOutput, calls=%fused_computation.1 | convolution fusion | flops 1034546176 | bytes 49246208 | tf_op jit(solution)/shard_map/tkgd,skd->kgts/dot_general | solution.py:104
  485.4 9.5 %convert_element_type.92 = bf16[1,8,640,768]{2,3,1,0:T(8,128)(2,1)} convert(f32[1,8,640,768]{2,3,1,0:T(8,128)} %get-tuple-element.4) | non-fusion elementwise | flops 3932160 | bytes 23592960 | tf_op jit(solution)/shard_map/convert_element_type | solution.py:85
  494.9 5.5 fusion.12
  500.4 17.3 %convolution_convert_fusion = bf16[640,8192]{1,0:T(8,128)(2,1)} fusion(bf16[640,1024]{0,1:T(8,128)(2,1)} %bitcast.105, bf16[1024,8192]{0,1:T(8,128)(2,1)} %bitcast.20), kind=kOutput, calls=%fused_computation.4 | convolution fusion | flops 10742661120 | bytes 28573696 | tf_op jit(solution)/shard_map/dot_general | solution.py:88
  517.7 2.5 slice_bitcast_fusion
  520.2 2.9 copy.49
  523.1 1.8 copy.58
  525.5 3.7 fusion.24
  529.2 16.0 %all_to_all.10 = bf16[32,4,256]{2,1,0:T(4,128)(2,1)S(1)} all-to-all(bf16[32,4,256]{2,1,0:T(4,128)(2,1)S(1)} %pad_maximum_fusion.3), channel_id=1, replica_groups=mesh['dp'=32,'mp'=4] {'dp'}, dimensions={0} | all-to-all | bytes 131072 | tf_op jit(solution)/shard_map/all_to_all | solution.py:23
  545.9 80.6 %reduce-scatter.2.cloned.1.call-done = bf16[640,2048]{1,0:T(8,128)(2,1)} async-done(((bf16[640,8192]{1,0:T(8,128)(2,1)}), bf16[640,2048]{1,0:T(8,128)(2,1)}) %reduce-scatter.2.cloned.1.call-update) | async-done | bytes 2621456 | tf_op jit(solution)/shard_map/reduce_scatter | solution.py:97
  (37 shorter events, 2.7 us)
Async XLA Ops:
  7.2 443.5 %all-gather.2.cloned.1.call-start = ((), (), s32[]{:S(2)}) async-start(), calls=%async_computation.4 | async-start | bytes 17301504 | tf_op jit(solution)/shard_map/all_gather | solution.py:93
  15.1 9.5 %copy-start.2 = (bf16[640,1024]{1,0:T(8,128)(2,1)S(1)}, bf16[640,1024]{1,0:T(8,128)(2,1)}, u32[]{:S(2)}) copy-start(bf16[640,1024]{1,0:T(8,128)(2,1)} %param.8) | copy-start | bytes 3932164
  15.1 485.2 %all-to-all-start = ((bf16[32,1024,256]{1,2,0:T(8,128)(2,1)}), bf16[32,1024,256]{1,2,0:T(8,128)(2,1)}, u32[]{:S(2)}, u32[]{:S(2)}) async-start(bf16[32,1024,256]{1,2,0:T(8,128)(2,1)} %stack.2), calls=%async_computation | async-start | bytes 33554432 | tf_op jit(solution)/shard_map/all_to_all | solution.py:12
  24.6 601.8 %reduce-scatter.2.cloned.1.call-start = ((), (), s32[]{:S(2)}) async-start(), calls=%async_computation.3 | async-start | bytes 13107200 | tf_op jit(solution)/shard_map/reduce_scatter | solution.py:97
  25.6 2.9 copy-start.3
  25.6 3.1 copy-start.5
  25.6 3.2 copy-start.4
  25.6 3.4 copy-start.6
  25.6 3.5 copy-start.7
  29.3 2.5 copy-start.1
  523.1 1.8 copy-start
Sparse Core Ops, SparseCore 0:
  9.6 441.0 all-gather.1
  517.8 108.5 reduce-scatter.1
